TPU v7x, 32 devices: a whole 2x2x4 slice. The times are simulated.
32 devices in a mesh: row: 8 (over z, y), col: 4 (over x, core).
Axes of the slice: x: 2, y: 2, z: 4, core: 2. Of those that a mesh axis runs over, the one named last changes fastest.
Arguments:
- signal: bfloat16 [8, 256, 512], P(None, 'row', 'col'), may hold values from -6 to 6
- filter_real: bfloat16 [8, 256, 512], P(None, 'row', 'col'), may hold values from -6 to 6
- filter_imag: bfloat16 [8, 256, 512], P(None, 'row', 'col'), may hold values from -6 to 6
- skip: float32 [8], replicated, may hold values from 0.5 to 1.5
Outputs:
- output: bfloat16 [8, 256, 512], P(None, 'row', 'col')
All inputs are finite; a program needn't handle non-finite values.
Results may differ from a plain program's by a relative error of at most 0.0064.
Values may be sent and summed in bfloat16 or wider, within the bound.
No kernel may reach another device: no remote copies, remote signals or barrier semaphores. Data moves between devices by JAX's collectives and lax.ppermute only.
A program may use at most 64 MiB of HBM per device.

v0:
```python
import math
import jax
import jax.numpy as jnp
from jax import lax
from jax.sharding import PartitionSpec as P


def phase_table(left_ids, right_ids, modulus):
    product = left_ids[:, None] * right_ids[None, :] % modulus
    angle = -2.0 * math.pi / modulus * product.astype(jnp.float32)
    return (jnp.cos(angle).astype(jnp.bfloat16), jnp.sin(angle).astype(jnp.bfloat16))


def twist_table(left_ids, right_ids, modulus):
    product = left_ids[:, None] * right_ids[None, :] % modulus
    angle = -2.0 * math.pi / modulus * product.astype(jnp.float32)
    return (jnp.cos(angle), jnp.sin(angle))


def column_product(series, phase):
    return jnp.einsum("crn,nk->crk", series, phase, preferred_element_type=jnp.float32)


def row_product(phase, series):
    return jnp.einsum("rn,cnj->crj", phase, series, preferred_element_type=jnp.float32)


def local(signal, filter_real, filter_imag, skip):
    channels, row_count, col_count = signal.shape
    first_len = row_count * lax.axis_size("row")
    second_len = col_count * lax.axis_size("col")
    seq_len = first_len * second_len
    row_offset = lax.axis_index("row") * row_count
    col_offset = lax.axis_index("col") * col_count
    own_rows = row_offset + jnp.arange(row_count, dtype=jnp.int32)
    own_cols = col_offset + jnp.arange(col_count, dtype=jnp.int32)
    twist_re, twist_im = twist_table(own_rows, own_cols, seq_len)
    pair_width = col_count // lax.axis_size("row")
    pair_cols = (
        col_offset + lax.axis_index("row") * pair_width + jnp.arange(pair_width, dtype=jnp.int32)
    )
    all_rows = jnp.arange(first_len, dtype=jnp.int32)
    full_re, full_im = phase_table(all_rows, all_rows, first_len)
    columns_whole = lax.all_to_all(signal, "row", split_axis=2, concat_axis=1, tiled=True)
    pair_b_re = row_product(full_re, columns_whole)
    pair_b_im = row_product(full_im, columns_whole)
    pair_tw_re, pair_tw_im = twist_table(all_rows, pair_cols, seq_len)
    pair_mix_re = (pair_b_re * pair_tw_re - pair_b_im * pair_tw_im).astype(jnp.bfloat16)
    pair_mix_im = (pair_b_re * pair_tw_im + pair_b_im * pair_tw_re).astype(jnp.bfloat16)
    mixed_re, mixed_im = (
        lax.all_to_all(pair_mix_re, "row", split_axis=1, concat_axis=2, tiled=True),
        lax.all_to_all(pair_mix_im, "row", split_axis=1, concat_axis=2, tiled=True),
    )
    pieces = (
        lax.all_gather(mixed_re, "col", axis=2, tiled=True),
        lax.all_gather(mixed_im, "col", axis=2, tiled=True),
    )
    amount = pieces[0].shape[2]
    phase_re, phase_im = phase_table(jnp.arange(amount, dtype=jnp.int32), own_cols, second_len)
    part_re, part_im = pieces
    new_re = column_product(part_re, phase_re) - column_product(part_im, phase_im)
    new_im = column_product(part_re, phase_im) + column_product(part_im, phase_re)
    spec_re = new_re
    spec_im = new_im
    prod_re = (spec_re * filter_real - spec_im * filter_imag).astype(jnp.bfloat16)
    prod_im = (spec_re * filter_imag + spec_im * filter_real).astype(jnp.bfloat16)
    pieces = (
        lax.all_gather(prod_re, "col", axis=2, tiled=True),
        lax.all_gather(prod_im, "col", axis=2, tiled=True),
    )
    amount = pieces[0].shape[2]
    phase_re, phase_im = phase_table(jnp.arange(amount, dtype=jnp.int32), own_cols, second_len)
    part_re, part_im = pieces
    new_re = column_product(part_re, phase_re) + column_product(part_im, phase_im)
    new_im = column_product(part_im, phase_re) - column_product(part_re, phase_im)
    unwound_re = (new_re * twist_re + new_im * twist_im).astype(jnp.bfloat16)
    unwound_im = (new_im * twist_re - new_re * twist_im).astype(jnp.bfloat16)
    pair_un_re, pair_un_im = (
        lax.all_to_all(unwound_re, "row", split_axis=2, concat_axis=1, tiled=True),
        lax.all_to_all(unwound_im, "row", split_axis=2, concat_axis=1, tiled=True),
    )
    pair_total = row_product(full_re, pair_un_re) + row_product(full_im, pair_un_im)
    pair_out = (
        pair_total / seq_len + skip[:, None, None] * columns_whole.astype(jnp.float32)
    ).astype(jnp.bfloat16)
    return lax.all_to_all(pair_out, "row", split_axis=1, concat_axis=2, tiled=True)


def solution(mesh):
    in_specs = (P(None, "row", "col"), P(None, "row", "col"), P(None, "row", "col"), P())
    out_specs = P(None, "row", "col")
    return jax.shard_map(local, mesh=mesh, in_specs=in_specs, out_specs=out_specs, check_vma=False)
```

profile of v0, /device:TPU:0, one launch (start us, length us, event | category | flops | bytes accessed | tf_op | source)
XLA Modules:
  0.0 107.6 jit_solution(13827530816031073000)
XLA Ops:
  0.0 1.0 copy.23
  1.0 0.9 reshape.142
  1.9 7.3 %all-to-all-start = ((bf16[8,2,2048]{2,1,0:T(2,128)(2,1)}), bf16[8,2,2048]{2,1,0:T(2,128)(2,1)S(1)}, u32[]{:S(2)}, u32[]{:S(2)}) async-start(bf16[8,2,2048]{2,1,0:T(2,128)(2,1)} %reshape.142), calls=%async_computation | async-start | bytes 131072 | tf_op jit(solution)/shard_map/all_to_all | solution.py:44
  9.4 6.7 %all-to-all-done = bf16[8,2,2048]{2,1,0:T(2,128)(2,1)S(1)} async-done(((bf16[8,2,2048]{2,1,0:T(2,128)(2,1)}), bf16[8,2,2048]{2,1,0:T(2,128)(2,1)S(1)}, u32[]{:S(2)}, u32[]{:S(2)}) %all-to-all-start) | async-done | bytes 65568 | tf_op jit(solution)/shard_map/all_to_all | solution.py:44
  16.2 0.2 reshape.143
  16.7 1.1 %fusion.38 = f32[256,128]{0,1:S(1)} fusion(bf16[256,128]{0,1:T(8,128)(2,1)S(1)} %bitcast.113), kind=kOutput, calls=%fused_computation.53 | convolution fusion | flops 17760256 | bytes 196608
  17.8 1.1 %fusion.37 = f32[256,128]{0,1:S(1)} fusion(bf16[256,128]{0,1:T(8,128)(2,1)S(1)} %bitcast.114), kind=kOutput, calls=%fused_computation.52 | convolution fusion | flops 17760256 | bytes 196608
  19.0 0.3 copy.26
  19.3 1.2 %reshape.144 = bf16[8,2,2048]{2,1,0:T(2,128)(2,1)} reshape(bf16[256,8,16]{2,1,0:T(8,128)(2,1)S(1)} %bitcast.96) | data formatting | bytes 131072
  20.5 3.4 %all-to-all-start.1 = ((bf16[8,2,2048]{2,1,0:T(2,128)(2,1)}), bf16[8,2,2048]{2,1,0:T(2,128)(2,1)S(1)}, u32[]{:S(2)}, u32[]{:S(2)}) async-start(bf16[8,2,2048]{2,1,0:T(2,128)(2,1)} %reshape.144), calls=%async_computation.1 | async-start | bytes 131072 | tf_op jit(solution)/shard_map/all_to_all | solution.py:51
  24.0 0.3 copy.29
  24.3 1.2 %reshape.146 = bf16[8,2,2048]{2,1,0:T(2,128)(2,1)} reshape(bf16[256,8,16]{2,1,0:T(8,128)(2,1)S(1)} %bitcast.97) | data formatting | bytes 131072
  25.5 5.2 %all-to-all-done.1 = bf16[8,2,2048]{2,1,0:T(2,128)(2,1)S(1)} async-done(((bf16[8,2,2048]{2,1,0:T(2,128)(2,1)}), bf16[8,2,2048]{2,1,0:T(2,128)(2,1)S(1)}, u32[]{:S(2)}, u32[]{:S(2)}) %all-to-all-start.1) | async-done | bytes 65568 | tf_op jit(solution)/shard_map/all_to_all | solution.py:51
  30.7 3.3 %all-to-all-start.2 = ((bf16[8,2,2048]{2,1,0:T(2,128)(2,1)}), bf16[8,2,2048]{2,1,0:T(2,128)(2,1)S(1)}, u32[]{:S(2)}, u32[]{:S(2)}) async-start(bf16[8,2,2048]{2,1,0:T(2,128)(2,1)} %reshape.146), calls=%async_computation.2 | async-start | bytes 131072 | tf_op jit(solution)/shard_map/all_to_all | solution.py:52
  34.0 0.4 reshape.145
  34.4 0.4 copy.27
  34.9 5.8 %all_gather.12 = bf16[8,32,512]{2,1,0:T(8,128)(2,1)S(1)} all-gather(bf16[8,32,128]{2,1,0:T(8,128)(2,1)S(1)} %copy.28), channel_id=1, replica_groups=mesh['row'=8,'col'=4] {'col'}, dimensions={2}, use_global_device_ids=true | all-gather | bytes 327680 | tf_op jit(solution)/shard_map/all_gather | solution.py:55
  40.8 1.2 %fusion.27 = f32[8,32,128]{2,1,0:T(8,128)S(1)} fusion(bf16[8,32,512]{2,1,0:T(8,128)(2,1)S(1)} %all_gather.12, s32[128]{0:T(128)S(1)} %iota_add_fusion.1), kind=kOutput, calls=%fused_computation.47 | convolution fusion | flops 34537472 | bytes 393728 | tf_op jit(solution)/shard_map/crn,nk->crk/dot_general | solution.py:21
  41.9 1.2 %fusion.35 = f32[8,32,128]{2,1,0:T(8,128)S(1)} fusion(bf16[8,32,512]{2,1,0:T(8,128)(2,1)S(1)} %all_gather.12, s32[128]{0:T(128)S(1)} %iota_add_fusion.1), kind=kOutput, calls=%fused_computation.50 | convolution fusion | flops 34537472 | bytes 393728 | tf_op jit(solution)/shard_map/crn,nk->crk/dot_general | solution.py:21
  43.1 0.4 reshape.147
  43.5 0.4 copy.30
  44.0 5.9 %all_gather.13 = bf16[8,32,512]{2,1,0:T(8,128)(2,1)S(1)} all-gather(bf16[8,32,128]{2,1,0:T(8,128)(2,1)S(1)} %copy.31), channel_id=1, replica_groups=mesh['row'=8,'col'=4] {'col'}, dimensions={2}, use_global_device_ids=true | all-gather | bytes 327680 | tf_op jit(solution)/shard_map/all_gather | solution.py:56
  49.9 1.2 %convolution_add_fusion.1 = f32[8,32,128]{2,1,0:T(8,128)S(1)} fusion(f32[8,32,128]{2,1,0:T(8,128)S(1)} %fusion.27, bf16[8,32,512]{2,1,0:T(8,128)(2,1)S(1)} %all_gather.13, s32[128]{0:T(128)S(1)} %iota_add_fusion.1), kind=kOutput, calls=%fused_computation.2 | convolution fusion | flops 34570240 | bytes 524800 | tf_op jit(solution)/shard_map/crn,nk->crk/dot_general | solution.py:21
  51.1 1.2 %fusion.17 = (bf16[8,32,128]{2,1,0:T(8,128)(2,1)S(1)}, bf16[8,32,128]{2,1,0:T(8,128)(2,1)S(1)}) fusion(bf16[8,32,128]{2,1,0:T(8,128)(2,1)S(1)} %copy-done, f32[8,32,128]{2,1,0:T(8,128)S(1)} %convolution_add_fusion.1, bf16[8,32,128]{2,1,0:T(8,128)(2,1)S(1)} %copy-done.1, f32[8,32,128]{2,1,0:T(8,128)S(1)} %fusion.35, bf16[8,32,512]{2,1,0:T(8,128)(2,1)S(1)} %all_gather.13, ...), kind=kOutput, calls=%fused_computation.36 | convolution fusion | flops 34897920 | bytes 786944 | tf_op jit(solution)/shard_map/crn,nk->crk/dot_general | solution.py:21
  52.3 6.1 %all_gather.14 = bf16[8,32,512]{2,1,0:T(8,128)(2,1)S(1)} all-gather(bf16[8,32,128]{2,1,0:T(8,128)(2,1)S(1)} %get-tuple-element.5), channel_id=1, replica_groups=mesh['row'=8,'col'=4] {'col'}, dimensions={2}, use_global_device_ids=true | all-gather | bytes 327680 | tf_op jit(solution)/shard_map/all_gather | solution.py:68
  58.4 1.2 %fusion.32 = f32[8,32,128]{2,1,0:T(8,128)S(1)} fusion(bf16[8,32,512]{2,1,0:T(8,128)(2,1)S(1)} %all_gather.14, s32[128]{0:T(128)S(1)} %iota_add_fusion.1), kind=kOutput, calls=%fused_computation.49 | convolution fusion | flops 34537472 | bytes 393728 | tf_op jit(solution)/shard_map/crn,nk->crk/dot_general | solution.py:21
  59.5 5.9 %all_gather.15 = bf16[8,32,512]{2,1,0:T(8,128)(2,1)S(1)} all-gather(bf16[8,32,128]{2,1,0:T(8,128)(2,1)S(1)} %get-tuple-element.6), channel_id=1, replica_groups=mesh['row'=8,'col'=4] {'col'}, dimensions={2}, use_global_device_ids=true | all-gather | bytes 327680 | tf_op jit(solution)/shard_map/all_gather | solution.py:69
  65.4 1.2 %fusion.30 = f32[8,32,128]{2,1,0:T(8,128)S(1)} fusion(bf16[8,32,512]{2,1,0:T(8,128)(2,1)S(1)} %all_gather.15, s32[128]{0:T(128)S(1)} %iota_add_fusion.1), kind=kOutput, calls=%fused_computation.48 | convolution fusion | flops 34537472 | bytes 393728 | tf_op jit(solution)/shard_map/crn,nk->crk/dot_general | solution.py:21
  66.6 1.2 %convolution_subtract_fusion = f32[8,32,128]{2,1,0:T(8,128)S(1)} fusion(f32[8,32,128]{2,1,0:T(8,128)S(1)} %fusion.30, bf16[8,32,512]{2,1,0:T(8,128)(2,1)S(1)} %all_gather.14, s32[128]{0:T(128)S(1)} %iota_add_fusion.1), kind=kOutput, calls=%fused_computation | convolution fusion | flops 34570240 | bytes 524800 | tf_op jit(solution)/shard_map/crn,nk->crk/dot_general | solution.py:21
  67.8 1.2 %subtract_convert_fusion = (bf16[8,32,128]{2,1,0:T(8,128)(2,1)S(1)}, bf16[8,32,128]{2,1,0:T(8,128)(2,1)S(1)}) fusion(f32[8,32,128]{2,1,0:T(8,128)S(1)} %convolution_subtract_fusion, f32[32,128]{1,0:T(8,128)S(1)} %get-tuple-element.12, f32[32,128]{1,0:T(8,128)S(1)} %get-tuple-element.11, f32[8,32,128]{2,1,0:T(8,128)S(1)} %fusion.32, ...), kind=kOutput, calls=%fused_computation.44 | convolution fusion | flops 34832384 | bytes 688640 | tf_op jit(solution)/shard_map/crn,nk->crk/dot_general | solution.py:21
  68.9 0.2 copy.35
  69.1 0.9 reshape.150
  70.1 5.9 %all-to-all-start.4 = ((bf16[8,2,2048]{2,1,0:T(2,128)(2,1)}), bf16[8,2,2048]{2,1,0:T(2,128)(2,1)S(1)}, u32[]{:S(2)}, u32[]{:S(2)}) async-start(bf16[8,2,2048]{2,1,0:T(2,128)(2,1)} %reshape.150), calls=%async_computation.4 | async-start | bytes 131072 | tf_op jit(solution)/shard_map/all_to_all | solution.py:80
  76.0 0.2 copy.32
  76.2 0.9 reshape.148
  77.1 5.8 %all-to-all-done.4 = bf16[8,2,2048]{2,1,0:T(2,128)(2,1)S(1)} async-done(((bf16[8,2,2048]{2,1,0:T(2,128)(2,1)}), bf16[8,2,2048]{2,1,0:T(2,128)(2,1)S(1)}, u32[]{:S(2)}, u32[]{:S(2)}) %all-to-all-start.4) | async-done | bytes 65568 | tf_op jit(solution)/shard_map/all_to_all | solution.py:80
  82.9 3.4 %all-to-all-start.3 = ((bf16[8,2,2048]{2,1,0:T(2,128)(2,1)}), bf16[8,2,2048]{2,1,0:T(2,128)(2,1)S(1)}, u32[]{:S(2)}, u32[]{:S(2)}) async-start(bf16[8,2,2048]{2,1,0:T(2,128)(2,1)} %reshape.148), calls=%async_computation.3 | async-start | bytes 131072 | tf_op jit(solution)/shard_map/all_to_all | solution.py:79
  86.3 0.2 reshape.151
  86.8 6.3 %all-to-all-done.3 = bf16[8,2,2048]{2,1,0:T(2,128)(2,1)S(1)} async-done(((bf16[8,2,2048]{2,1,0:T(2,128)(2,1)}), bf16[8,2,2048]{2,1,0:T(2,128)(2,1)S(1)}, u32[]{:S(2)}, u32[]{:S(2)}) %all-to-all-start.3) | async-done | bytes 65568 | tf_op jit(solution)/shard_map/all_to_all | solution.py:79
  93.1 0.2 reshape.149
  93.7 1.1 %fusion.23 = f32[8,16,256]{2,1,0:T(8,128)S(1)} fusion(bf16[8,256,16]{1,2,0:T(8,128)(2,1)S(1)} %all_to_all.93), kind=kOutput, calls=%fused_computation.42 | convolution fusion | flops 17760256 | bytes 196608 | tf_op jit(solution)/shard_map/rn,cnj->crj/dot_general | solution.py:25
  94.8 1.1 %fusion.3 = bf16[8,256,16]{1,2,0:T(8,128)(2,1)S(1)} fusion(f32[8,16,256]{2,1,0:T(8,128)S(1)} %fusion.23, bf16[8,256,16]{1,2,0:T(8,128)(2,1)S(1)} %all_to_all.97, bf16[8,256,16]{1,2,0:T(8,128)(2,1)S(1)} %all_to_all.81, f32[8]{0:T(128)S(1)} %copy-done.2), kind=kOutput, calls=%fused_computation.8 | convolution fusion | flops 17956864 | bytes 327712 | tf_op jit(solution)/shard_map/rn,cnj->crj/dot_general | solution.py:25
  95.9 0.3 copy.38
  96.2 0.5 reshape.152
  96.8 9.3 %all_to_all.108 = bf16[8,2,2048]{2,1,0:T(2,128)(2,1)S(1)} all-to-all(bf16[8,2,2048]{2,1,0:T(2,128)(2,1)S(1)} %reshape.152), channel_id=1, replica_groups=mesh['row'=8,'col'=4] {'row'}, dimensions={0} | all-to-all | bytes 131072 | tf_op jit(solution)/shard_map/all_to_all | solution.py:86
  106.1 0.4 reshape.153
  106.4 0.4 copy.39
  106.8 0.8 copy.40
  (21 shorter events, 1.7 us)
Async XLA Ops:
  1.9 14.2 %all-to-all-start = ((bf16[8,2,2048]{2,1,0:T(2,128)(2,1)}), bf16[8,2,2048]{2,1,0:T(2,128)(2,1)S(1)}, u32[]{:S(2)}, u32[]{:S(2)}) async-start(bf16[8,2,2048]{2,1,0:T(2,128)(2,1)} %reshape.142), calls=%async_computation | async-start | bytes 131072 | tf_op jit(solution)/shard_map/all_to_all | solution.py:44
  20.5 10.2 %all-to-all-start.1 = ((bf16[8,2,2048]{2,1,0:T(2,128)(2,1)}), bf16[8,2,2048]{2,1,0:T(2,128)(2,1)S(1)}, u32[]{:S(2)}, u32[]{:S(2)}) async-start(bf16[8,2,2048]{2,1,0:T(2,128)(2,1)} %reshape.144), calls=%async_computation.1 | async-start | bytes 131072 | tf_op jit(solution)/shard_map/all_to_all | solution.py:51
  30.7 12.4 %all-to-all-start.2 = ((bf16[8,2,2048]{2,1,0:T(2,128)(2,1)}), bf16[8,2,2048]{2,1,0:T(2,128)(2,1)S(1)}, u32[]{:S(2)}, u32[]{:S(2)}) async-start(bf16[8,2,2048]{2,1,0:T(2,128)(2,1)} %reshape.146), calls=%async_computation.2 | async-start | bytes 131072 | tf_op jit(solution)/shard_map/all_to_all | solution.py:52
  49.9 1.2 %copy-start = (bf16[8,32,128]{2,1,0:T(8,128)(2,1)S(1)}, bf16[8,32,128]{2,1,0:T(8,128)(2,1)}, u32[]{:S(2)}) copy-start(bf16[8,32,128]{2,1,0:T(8,128)(2,1)} %param.5) | copy-start | bytes 196612
  49.9 1.2 %copy-start.1 = (bf16[8,32,128]{2,1,0:T(8,128)(2,1)S(1)}, bf16[8,32,128]{2,1,0:T(8,128)(2,1)}, u32[]{:S(2)}) copy-start(bf16[8,32,128]{2,1,0:T(8,128)(2,1)} %param.6) | copy-start | bytes 196612
  70.1 12.8 %all-to-all-start.4 = ((bf16[8,2,2048]{2,1,0:T(2,128)(2,1)}), bf16[8,2,2048]{2,1,0:T(2,128)(2,1)S(1)}, u32[]{:S(2)}, u32[]{:S(2)}) async-start(bf16[8,2,2048]{2,1,0:T(2,128)(2,1)} %reshape.150), calls=%async_computation.4 | async-start | bytes 131072 | tf_op jit(solution)/shard_map/all_to_all | solution.py:80
  82.9 10.2 %all-to-all-start.3 = ((bf16[8,2,2048]{2,1,0:T(2,128)(2,1)}), bf16[8,2,2048]{2,1,0:T(2,128)(2,1)S(1)}, u32[]{:S(2)}, u32[]{:S(2)}) async-start(bf16[8,2,2048]{2,1,0:T(2,128)(2,1)} %reshape.148), calls=%async_computation.3 | async-start | bytes 131072 | tf_op jit(solution)/shard_map/all_to_all | solution.py:79
  93.6 1.1 %copy-start.2 = (f32[8]{0:T(128)S(1)}, f32[8]{0:T(128)}, u32[]{:S(2)}) copy-start(f32[8]{0:T(128)} %param.7) | copy-start | bytes 100
where the time goes:
time: 108 us
  blocking collectives  33 us (31%)
  waiting for transfers between devices  24 us (22%)
  starting transfers between devices  23.3 us (22%)
  matrix products  13.7 us (13%)
  local copies, waits for them, and re-layouts  12.9 us (12%)
    all_to_all x1, blocking collectives, local(): lax.all_to_all(pair_out, 'row', split_axis=1, concat_axis=2, tiled=True)  9.29 us
    dot_general x8, matrix products, column_product(): jnp.einsum('crn,nk->crk', series, phase, preferred_element_type=jnp.float32)  9.28 us
    unnamed x19, local copies, waits for them, and re-layouts  8.34 us
    all_to_all x1, starting transfers between devices, local(): lax.all_to_all(signal, 'row', split_axis=2, concat_axis=1, tiled=True)  7.31 us
    all_to_all x1, waiting for transfers between devices, local(): lax.all_to_all(signal, 'row', split_axis=2, concat_axis=1, tiled=True)  6.72 us
    all_to_all x1, waiting for transfers between devices, local(): lax.all_to_all(unwound_re, 'row', split_axis=2, concat_axis=1, tiled=True)  6.29 us
    all_gather x1, blocking collectives, local(): lax.all_gather(prod_re, 'col', axis=2, tiled=True)  6.09 us
    all_to_all x1, starting transfers between devices, local(): lax.all_to_all(unwound_im, 'row', split_axis=2, concat_axis=1, tiled=True)  5.93 us
  transfers between devices with their start and end apart: 5, of which 4 were waited for; matrix products, arithmetic and copies ran while one was open for 6% of the time, Pallas kernels for 0%

commit v1 on v0

--- a/solution.py
+++ b/solution.py
@@ -41,7 +41,19 @@
     )
     all_rows = jnp.arange(first_len, dtype=jnp.int32)
     full_re, full_im = phase_table(all_rows, all_rows, first_len)
-    columns_whole = lax.all_to_all(signal, "row", split_axis=2, concat_axis=1, tiled=True)
+    ways, here = (lax.axis_size("row"), lax.axis_index("row"))
+    width = signal.shape[2] // ways
+    dims = list(signal.shape)
+    dims[2] = width
+    height = dims[1]
+    dims[1] = height * ways
+    full = jnp.zeros(dims, signal.dtype)
+    for mask in range(ways):
+        part = lax.dynamic_slice_in_dim(signal, (here ^ mask) * width, width, axis=2)
+        if mask:
+            part = lax.ppermute(part, "row", [(d, d ^ mask) for d in range(ways)])
+        full = lax.dynamic_update_slice_in_dim(full, part, (here ^ mask) * height, axis=1)
+    columns_whole = full
     pair_b_re = row_product(full_re, columns_whole)
     pair_b_im = row_product(full_im, columns_whole)
     pair_tw_re, pair_tw_im = twist_table(all_rows, pair_cols, seq_len)

time: 108 us -> 118 us (1.093)
  starting transfers between devices: 23.3 us -> 31.7 us
  local copies, waits for them, and re-layouts: 12.9 us -> 20.9 us
  waiting for transfers between devices: 24 us -> 17.1 us
    ppermute x0 -> x7, starting transfers between devices: none -> 12.9 us  [local(): part = lax.ppermute(part, 'row', [(d, d ^ mask) for d in range(ways)])]
    dynamic_update_slice x0 -> x8, local copies, waits for them, and re-layouts: none -> 8.64 us  [local(): lax.dynamic_update_slice_in_dim(full, part, (here ^ mask) * height, axis=1)]
    all_to_all x1 -> x0, starting transfers between devices: 7.31 us -> none  [local(): lax.all_to_all(signal, 'row', split_axis=2, concat_axis=1, tiled=True)]
    all_to_all x1 -> x0, waiting for transfers between devices: 6.72 us -> none  [local(): lax.all_to_all(signal, 'row', split_axis=2, concat_axis=1, tiled=True)]
    all_to_all x1, starting transfers between devices: 3.35 us -> 5.95 us  [local(): lax.all_to_all(pair_mix_re, 'row', split_axis=1, concat_axis=2, tiled=True)]
    dot_general x2 -> x4, matrix products: 2.21 us -> 4.44 us  [row_product(): jnp.einsum('rn,cnj->crj', phase, series, preferred_element_type=jnp.float32)]
    unnamed x2 -> x0, matrix products: 2.21 us -> none
    unnamed x19 -> x26, local copies, waits for them, and re-layouts: 8.34 us -> 7.81 us
  transfers between devices with their start and end apart: 5 -> 11, of which waited for: 4 -> 3; matrix products, arithmetic and copies ran while one was open for 6% -> 12% of each run, Pallas kernels for 0% -> 0%
where the time goes in v1:
time: 118 us; the launch traced here: 117 us
  blocking collectives  33 us (28%)
  starting transfers between devices  31.7 us (27%)
  local copies, waits for them, and re-layouts  20.9 us (18%)
  waiting for transfers between devices  17.1 us (14%)
  matrix products  13.7 us (12%)
    ppermute x7, starting transfers between devices, local(): part = lax.ppermute(part, 'row', [(d, d ^ mask) for d in range(ways)])  12.9 us
    all_to_all x1, blocking collectives, local(): lax.all_to_all(pair_out, 'row', split_axis=1, concat_axis=2, tiled=True)  9.29 us
    dot_general x8, matrix products, column_product(): jnp.einsum('crn,nk->crk', series, phase, preferred_element_type=jnp.float32)  9.27 us
    dynamic_update_slice x8, local copies, waits for them, and re-layouts, local(): lax.dynamic_update_slice_in_dim(full, part, (here ^ mask) * height, axis=1)  8.64 us
    unnamed x26, local copies, waits for them, and re-layouts  7.81 us
    all_to_all x1, waiting for transfers between devices, local(): lax.all_to_all(unwound_re, 'row', split_axis=2, concat_axis=1, tiled=True)  6.07 us
    all_gather x1, blocking collectives, local(): lax.all_gather(mixed_re, 'col', axis=2, tiled=True)  5.99 us
    all_to_all x1, starting transfers between devices, local(): lax.all_to_all(pair_mix_re, 'row', split_axis=1, concat_axis=2, tiled=True)  5.95 us
  transfers between devices with their start and end apart: 11, of which 3 were waited for; matrix products, arithmetic and copies ran while one was open for 12% of the time, Pallas kernels for 0%

profile of v1, /device:TPU:0, one launch (start us, length us, event | category | flops | bytes accessed | tf_op | source)
XLA Modules:
  0.0 117.2 jit_solution(959052607926505279)
XLA Ops:
  0.0 0.8 copy-done
  1.2 3.1 %collective-permute-start = (bf16[8,32,16]{1,2,0:T(8,128)(2,1)S(1)}, bf16[8,32,16]{1,2,0:T(8,128)(2,1)S(1)}, u32[]{:S(2)}, u32[]{:S(2)}) collective-permute-start(bf16[8,32,16]{1,2,0:T(8,128)(2,1)S(1)} %copy.62), channel_id=1, source_target_pairs={{0,4},{4,0},{8,12},{12,8},{16,20},{20,16},{24,28},{28,24},{1,5},{5... | collective-permute-start | bytes 24584 | tf_op jit(solution)/shard_map/ppermute | solution.py:54
  4.3 1.6 %collective-permute-start.1 = (bf16[8,32,16]{1,2,0:T(8,128)(2,1)S(1)}, bf16[8,32,16]{1,2,0:T(8,128)(2,1)S(1)}, u32[]{:S(2)}, u32[]{:S(2)}) collective-permute-start(bf16[8,32,16]{1,2,0:T(8,128)(2,1)S(1)} %copy.63), channel_id=1, source_target_pairs={{0,8},{4,12},{8,0},{12,4},{16,24},{20,28},{24,16},{28,20},{1,9},{5... | collective-permute-start | bytes 24584 | tf_op jit(solution)/shard_map/ppermute | solution.py:54
  6.2 3.0 %collective-permute-start.3 = (bf16[8,32,16]{1,2,0:T(8,128)(2,1)S(1)}, bf16[8,32,16]{1,2,0:T(8,128)(2,1)S(1)}, u32[]{:S(2)}, u32[]{:S(2)}) collective-permute-start(bf16[8,32,16]{1,2,0:T(8,128)(2,1)S(1)} %copy.65), channel_id=1, source_target_pairs={{0,16},{4,20},{8,24},{12,28},{16,0},{20,4},{24,8},{28,12},{1,17},{... | collective-permute-start | bytes 24584 | tf_op jit(solution)/shard_map/ppermute | solution.py:54
  9.3 1.4 %collective-permute-start.4 = (bf16[8,32,16]{1,2,0:T(8,128)(2,1)S(1)}, bf16[8,32,16]{1,2,0:T(8,128)(2,1)S(1)}, u32[]{:S(2)}, u32[]{:S(2)}) collective-permute-start(bf16[8,32,16]{1,2,0:T(8,128)(2,1)S(1)} %copy.66), channel_id=1, source_target_pairs={{0,20},{4,16},{8,28},{12,24},{16,4},{20,0},{24,12},{28,8},{1,21},{... | collective-permute-start | bytes 24584 | tf_op jit(solution)/shard_map/ppermute | solution.py:54
  11.1 3.7 %collective-permute-start.5 = (bf16[8,32,16]{1,2,0:T(8,128)(2,1)S(1)}, bf16[8,32,16]{1,2,0:T(8,128)(2,1)S(1)}, u32[]{:S(2)}, u32[]{:S(2)}) collective-permute-start(bf16[8,32,16]{1,2,0:T(8,128)(2,1)S(1)} %copy.67), channel_id=1, source_target_pairs={{0,24},{4,28},{8,16},{12,20},{16,8},{20,12},{24,0},{28,4},{1,25},{... | collective-permute-start | bytes 24584 | tf_op jit(solution)/shard_map/ppermute | solution.py:54
  15.2 1.4 %dynamic_update_slice.25 = bf16[8,256,16]{1,2,0:T(8,128)(2,1)S(1)} dynamic-update-slice(bf16[8,256,16]{1,2,0:T(8,128)(2,1)S(1)} %dynamic_update_slice.24, bf16[8,32,16]{1,2,0:T(8,128)(2,1)S(1)} %collective-permute-done, s32[]{:T(128)} %constant.72.clone.1, s32[]{:T(128)S(6)} %select_n.98, s32[]{:T(128)} %constant.72.clone.1) | dynamic-update-slice | bytes 16388 | tf_op jit(solution)/shard_map/dynamic_update_slice | solution.py:55
  16.6 1.4 %dynamic_update_slice.26 = bf16[8,256,16]{1,2,0:T(8,128)(2,1)S(1)} dynamic-update-slice(bf16[8,256,16]{1,2,0:T(8,128)(2,1)S(1)} %dynamic_update_slice.25, bf16[8,32,16]{1,2,0:T(8,128)(2,1)S(1)} %collective-permute-done.1, s32[]{:T(128)} %constant.72.clone.1, s32[]{:T(128)S(6)} %select_n.100, s32[]{:T(128)} %constant.72.clone.1) | dynamic-update-slice | bytes 16388 | tf_op jit(solution)/shard_map/dynamic_update_slice | solution.py:55
  18.0 1.4 %dynamic_update_slice.27 = bf16[8,256,16]{1,2,0:T(8,128)(2,1)S(1)} dynamic-update-slice(bf16[8,256,16]{1,2,0:T(8,128)(2,1)S(1)} %dynamic_update_slice.26, bf16[8,32,16]{1,2,0:T(8,128)(2,1)S(1)} %collective-permute-done.2, s32[]{:T(128)} %constant.72.clone.1, s32[]{:T(128)S(6)} %select_n.102, s32[]{:T(128)} %constant.72.clone.1) | dynamic-update-slice | bytes 16388 | tf_op jit(solution)/shard_map/dynamic_update_slice | solution.py:55
  19.6 1.3 %dynamic_update_slice.29 = bf16[8,256,16]{1,2,0:T(8,128)(2,1)S(1)} dynamic-update-slice(bf16[8,256,16]{1,2,0:T(8,128)(2,1)S(1)} %dynamic_update_slice.28, bf16[8,32,16]{1,2,0:T(8,128)(2,1)S(1)} %collective-permute-done.4, s32[]{:T(128)} %constant.72.clone.1, s32[]{:T(128)S(6)} %select_n.106, s32[]{:T(128)} %constant.72.clone.1) | dynamic-update-slice | bytes 16388 | tf_op jit(solution)/shard_map/dynamic_update_slice | solution.py:55
  21.0 1.3 %dynamic_update_slice.30 = bf16[8,256,16]{1,2,0:T(8,128)(2,1)S(1)} dynamic-update-slice(bf16[8,256,16]{1,2,0:T(8,128)(2,1)S(1)} %dynamic_update_slice.29, bf16[8,32,16]{1,2,0:T(8,128)(2,1)S(1)} %collective-permute-done.5, s32[]{:T(128)} %constant.72.clone.1, s32[]{:T(128)S(6)} %select_n.108, s32[]{:T(128)} %constant.72.clone.1) | dynamic-update-slice | bytes 16388 | tf_op jit(solution)/shard_map/dynamic_update_slice | solution.py:55
  22.4 1.3 %dynamic_update_slice.31 = bf16[8,256,16]{1,2,0:T(8,128)(2,1)S(1)} dynamic-update-slice(bf16[8,256,16]{1,2,0:T(8,128)(2,1)S(1)} %dynamic_update_slice.30, bf16[8,32,16]{1,2,0:T(8,128)(2,1)S(1)} %collective-permute-done.6, s32[]{:T(128)} %constant.72.clone.1, s32[]{:T(128)S(6)} %select_n.110, s32[]{:T(128)} %constant.72.clone.1) | dynamic-update-slice | bytes 16388 | tf_op jit(solution)/shard_map/dynamic_update_slice | solution.py:55
  23.7 1.1 convolution_bitcast_fusion.1
  24.8 1.1 add_convert_fusion.2
  26.3 1.2 %reshape.138 = bf16[8,2,2048]{2,1,0:T(2,128)(2,1)} reshape(bf16[256,8,16]{2,1,0:T(8,128)(2,1)S(1)} %bitcast.84) | data formatting | bytes 131072
  27.4 6.0 %all-to-all-start = ((bf16[8,2,2048]{2,1,0:T(2,128)(2,1)}), bf16[8,2,2048]{2,1,0:T(2,128)(2,1)S(1)}, u32[]{:S(2)}, u32[]{:S(2)}) async-start(bf16[8,2,2048]{2,1,0:T(2,128)(2,1)} %reshape.138), calls=%async_computation | async-start | bytes 131072 | tf_op jit(solution)/shard_map/all_to_all | solution.py:63
  33.9 1.2 %reshape.140 = bf16[8,2,2048]{2,1,0:T(2,128)(2,1)} reshape(bf16[256,8,16]{2,1,0:T(8,128)(2,1)S(1)} %bitcast.85) | data formatting | bytes 131072
  35.0 5.3 %all-to-all-done = bf16[8,2,2048]{2,1,0:T(2,128)(2,1)S(1)} async-done(((bf16[8,2,2048]{2,1,0:T(2,128)(2,1)}), bf16[8,2,2048]{2,1,0:T(2,128)(2,1)S(1)}, u32[]{:S(2)}, u32[]{:S(2)}) %all-to-all-start) | async-done | bytes 65568 | tf_op jit(solution)/shard_map/all_to_all | solution.py:63
  40.3 3.3 %all-to-all-start.1 = ((bf16[8,2,2048]{2,1,0:T(2,128)(2,1)}), bf16[8,2,2048]{2,1,0:T(2,128)(2,1)S(1)}, u32[]{:S(2)}, u32[]{:S(2)}) async-start(bf16[8,2,2048]{2,1,0:T(2,128)(2,1)} %reshape.140), calls=%async_computation.1 | async-start | bytes 131072 | tf_op jit(solution)/shard_map/all_to_all | solution.py:64
  43.7 0.4 reshape.139
  44.0 0.4 copy.45
  44.6 6.0 %all_gather.12 = bf16[8,32,512]{2,1,0:T(8,128)(2,1)S(1)} all-gather(bf16[8,32,128]{2,1,0:T(8,128)(2,1)S(1)} %copy.46), channel_id=1, replica_groups=mesh['row'=8,'col'=4] {'col'}, dimensions={2}, use_global_device_ids=true | all-gather | bytes 327680 | tf_op jit(solution)/shard_map/all_gather | solution.py:67
  50.6 1.2 fusion.24
  51.7 1.2 fusion.32
  52.9 0.4 reshape.141
  53.3 0.4 copy.48
  53.8 5.9 %all_gather.13 = bf16[8,32,512]{2,1,0:T(8,128)(2,1)S(1)} all-gather(bf16[8,32,128]{2,1,0:T(8,128)(2,1)S(1)} %copy.49), channel_id=1, replica_groups=mesh['row'=8,'col'=4] {'col'}, dimensions={2}, use_global_device_ids=true | all-gather | bytes 327680 | tf_op jit(solution)/shard_map/all_gather | solution.py:68
  59.7 1.2 convolution_add_fusion.1
  60.9 1.2 %fusion.15 = (bf16[8,32,128]{2,1,0:T(8,128)(2,1)S(1)}, bf16[8,32,128]{2,1,0:T(8,128)(2,1)S(1)}) fusion(bf16[8,32,128]{2,1,0:T(8,128)(2,1)S(1)} %copy-done.1, f32[8,32,128]{2,1,0:T(8,128)S(1)} %convolution_add_fusion.1, bf16[8,32,128]{2,1,0:T(8,128)(2,1)S(1)} %copy-done.2, f32[8,32,128]{2,1,0:T(8,128)S(1)} %fusion.32, ...), kind=kOutput, calls=%fused_computation.36 | convolution fusion | flops 34897920 | bytes 786944 | tf_op jit(solution)/shard_map/crn,nk->crk/dot_general | solution.py:21
  62.1 5.9 %all_gather.14 = bf16[8,32,512]{2,1,0:T(8,128)(2,1)S(1)} all-gather(bf16[8,32,128]{2,1,0:T(8,128)(2,1)S(1)} %get-tuple-element.5), channel_id=1, replica_groups=mesh['row'=8,'col'=4] {'col'}, dimensions={2}, use_global_device_ids=true | all-gather | bytes 327680 | tf_op jit(solution)/shard_map/all_gather | solution.py:80
  68.0 1.2 fusion.29
  69.1 5.9 %all_gather.15 = bf16[8,32,512]{2,1,0:T(8,128)(2,1)S(1)} all-gather(bf16[8,32,128]{2,1,0:T(8,128)(2,1)S(1)} %get-tuple-element.6), channel_id=1, replica_groups=mesh['row'=8,'col'=4] {'col'}, dimensions={2}, use_global_device_ids=true | all-gather | bytes 327680 | tf_op jit(solution)/shard_map/all_gather | solution.py:81
  75.1 1.2 fusion.27
  76.2 1.2 convolution_subtract_fusion
  77.4 1.2 %subtract_convert_fusion = (bf16[8,32,128]{2,1,0:T(8,128)(2,1)S(1)}, bf16[8,32,128]{2,1,0:T(8,128)(2,1)S(1)}) fusion(f32[8,32,128]{2,1,0:T(8,128)S(1)} %convolution_subtract_fusion, f32[32,128]{1,0:T(8,128)S(1)} %get-tuple-element.20, f32[32,128]{1,0:T(8,128)S(1)} %get-tuple-element.19, f32[8,32,128]{2,1,0:T(8,128)S(1)} %fusion.29, ...), kind=kOutput, calls=%fused_computation.44 | convolution fusion | flops 34832384 | bytes 688640 | tf_op jit(solution)/shard_map/crn,nk->crk/dot_general | solution.py:21
  78.8 0.9 reshape.144
  79.7 5.9 %all-to-all-start.3 = ((bf16[8,2,2048]{2,1,0:T(2,128)(2,1)}), bf16[8,2,2048]{2,1,0:T(2,128)(2,1)S(1)}, u32[]{:S(2)}, u32[]{:S(2)}) async-start(bf16[8,2,2048]{2,1,0:T(2,128)(2,1)} %reshape.144), calls=%async_computation.3 | async-start | bytes 131072 | tf_op jit(solution)/shard_map/all_to_all | solution.py:92
  85.8 0.9 reshape.142
  86.7 5.8 %all-to-all-done.3 = bf16[8,2,2048]{2,1,0:T(2,128)(2,1)S(1)} async-done(((bf16[8,2,2048]{2,1,0:T(2,128)(2,1)}), bf16[8,2,2048]{2,1,0:T(2,128)(2,1)S(1)}, u32[]{:S(2)}, u32[]{:S(2)}) %all-to-all-start.3) | async-done | bytes 65568 | tf_op jit(solution)/shard_map/all_to_all | solution.py:92
  92.5 3.6 %all-to-all-start.2 = ((bf16[8,2,2048]{2,1,0:T(2,128)(2,1)}), bf16[8,2,2048]{2,1,0:T(2,128)(2,1)S(1)}, u32[]{:S(2)}, u32[]{:S(2)}) async-start(bf16[8,2,2048]{2,1,0:T(2,128)(2,1)} %reshape.142), calls=%async_computation.2 | async-start | bytes 131072 | tf_op jit(solution)/shard_map/all_to_all | solution.py:91
  96.6 6.1 %all-to-all-done.2 = bf16[8,2,2048]{2,1,0:T(2,128)(2,1)S(1)} async-done(((bf16[8,2,2048]{2,1,0:T(2,128)(2,1)}), bf16[8,2,2048]{2,1,0:T(2,128)(2,1)S(1)}, u32[]{:S(2)}, u32[]{:S(2)}) %all-to-all-start.2) | async-done | bytes 65568 | tf_op jit(solution)/shard_map/all_to_all | solution.py:91
  103.3 1.1 fusion.38
  104.4 1.1 add_convert_fusion
  105.8 0.5 reshape.146
  106.4 9.3 %all_to_all.90 = bf16[8,2,2048]{2,1,0:T(2,128)(2,1)S(1)} all-to-all(bf16[8,2,2048]{2,1,0:T(2,128)(2,1)S(1)} %reshape.146), channel_id=1, replica_groups=mesh['row'=8,'col'=4] {'row'}, dimensions={0} | all-to-all | bytes 131072 | tf_op jit(solution)/shard_map/all_to_all | solution.py:98
  115.7 0.4 reshape.147
  116.0 0.4 copy.57
  116.4 0.8 copy.58
  (47 shorter events, 4.6 us)
Async XLA Ops:
  0.0 0.8 copy-start
  1.2 9.9 %collective-permute-start = (bf16[8,32,16]{1,2,0:T(8,128)(2,1)S(1)}, bf16[8,32,16]{1,2,0:T(8,128)(2,1)S(1)}, u32[]{:S(2)}, u32[]{:S(2)}) collective-permute-start(bf16[8,32,16]{1,2,0:T(8,128)(2,1)S(1)} %copy.62), channel_id=1, source_target_pairs={{0,4},{4,0},{8,12},{12,8},{16,20},{20,16},{24,28},{28,24},{1,5},{5... | collective-permute-start | bytes 24584 | tf_op jit(solution)/shard_map/ppermute | solution.py:54
  4.3 10.4 %collective-permute-start.1 = (bf16[8,32,16]{1,2,0:T(8,128)(2,1)S(1)}, bf16[8,32,16]{1,2,0:T(8,128)(2,1)S(1)}, u32[]{:S(2)}, u32[]{:S(2)}) collective-permute-start(bf16[8,32,16]{1,2,0:T(8,128)(2,1)S(1)} %copy.63), channel_id=1, source_target_pairs={{0,8},{4,12},{8,0},{12,4},{16,24},{20,28},{24,16},{28,20},{1,9},{5... | collective-permute-start | bytes 24584 | tf_op jit(solution)/shard_map/ppermute | solution.py:54
  6.0 11.9 %collective-permute-start.2 = (bf16[8,32,16]{1,2,0:T(8,128)(2,1)S(1)}, bf16[8,32,16]{1,2,0:T(8,128)(2,1)S(1)}, u32[]{:S(2)}, u32[]{:S(2)}) collective-permute-start(bf16[8,32,16]{1,2,0:T(8,128)(2,1)S(1)} %copy.64), channel_id=1, source_target_pairs={{0,12},{4,8},{8,4},{12,0},{16,28},{20,24},{24,20},{28,16},{1,13},{... | collective-permute-start | bytes 24584 | tf_op jit(solution)/shard_map/ppermute | solution.py:54
  6.2 13.1 %collective-permute-start.3 = (bf16[8,32,16]{1,2,0:T(8,128)(2,1)S(1)}, bf16[8,32,16]{1,2,0:T(8,128)(2,1)S(1)}, u32[]{:S(2)}, u32[]{:S(2)}) collective-permute-start(bf16[8,32,16]{1,2,0:T(8,128)(2,1)S(1)} %copy.65), channel_id=1, source_target_pairs={{0,16},{4,20},{8,24},{12,28},{16,0},{20,4},{24,8},{28,12},{1,17},{... | collective-permute-start | bytes 24584 | tf_op jit(solution)/shard_map/ppermute | solution.py:54
  9.3 10.3 %collective-permute-start.4 = (bf16[8,32,16]{1,2,0:T(8,128)(2,1)S(1)}, bf16[8,32,16]{1,2,0:T(8,128)(2,1)S(1)}, u32[]{:S(2)}, u32[]{:S(2)}) collective-permute-start(bf16[8,32,16]{1,2,0:T(8,128)(2,1)S(1)} %copy.66), channel_id=1, source_target_pairs={{0,20},{4,16},{8,28},{12,24},{16,4},{20,0},{24,12},{28,8},{1,21},{... | collective-permute-start | bytes 24584 | tf_op jit(solution)/shard_map/ppermute | solution.py:54
  11.1 9.9 %collective-permute-start.5 = (bf16[8,32,16]{1,2,0:T(8,128)(2,1)S(1)}, bf16[8,32,16]{1,2,0:T(8,128)(2,1)S(1)}, u32[]{:S(2)}, u32[]{:S(2)}) collective-permute-start(bf16[8,32,16]{1,2,0:T(8,128)(2,1)S(1)} %copy.67), channel_id=1, source_target_pairs={{0,24},{4,28},{8,16},{12,20},{16,8},{20,12},{24,0},{28,4},{1,25},{... | collective-permute-start | bytes 24584 | tf_op jit(solution)/shard_map/ppermute | solution.py:54
  14.8 7.6 %collective-permute-start.6 = (bf16[8,32,16]{1,2,0:T(8,128)(2,1)S(1)}, bf16[8,32,16]{1,2,0:T(8,128)(2,1)S(1)}, u32[]{:S(2)}, u32[]{:S(2)}) collective-permute-start(bf16[8,32,16]{1,2,0:T(8,128)(2,1)S(1)} %copy.68), channel_id=1, source_target_pairs={{0,28},{4,24},{8,20},{12,16},{16,12},{20,8},{24,4},{28,0},{1,29},{... | collective-permute-start | bytes 24584 | tf_op jit(solution)/shard_map/ppermute | solution.py:54
  27.4 12.9 %all-to-all-start = ((bf16[8,2,2048]{2,1,0:T(2,128)(2,1)}), bf16[8,2,2048]{2,1,0:T(2,128)(2,1)S(1)}, u32[]{:S(2)}, u32[]{:S(2)}) async-start(bf16[8,2,2048]{2,1,0:T(2,128)(2,1)} %reshape.138), calls=%async_computation | async-start | bytes 131072 | tf_op jit(solution)/shard_map/all_to_all | solution.py:63
  40.3 12.6 %all-to-all-start.1 = ((bf16[8,2,2048]{2,1,0:T(2,128)(2,1)}), bf16[8,2,2048]{2,1,0:T(2,128)(2,1)S(1)}, u32[]{:S(2)}, u32[]{:S(2)}) async-start(bf16[8,2,2048]{2,1,0:T(2,128)(2,1)} %reshape.140), calls=%async_computation.1 | async-start | bytes 131072 | tf_op jit(solution)/shard_map/all_to_all | solution.py:64
  59.7 1.2 copy-start.1
  59.7 1.2 %copy-start.2 = (bf16[8,32,128]{2,1,0:T(8,128)(2,1)S(1)}, bf16[8,32,128]{2,1,0:T(8,128)(2,1)}, u32[]{:S(2)}) copy-start(bf16[8,32,128]{2,1,0:T(8,128)(2,1)} %param.6) | copy-start | bytes 196612
  79.7 12.8 %all-to-all-start.3 = ((bf16[8,2,2048]{2,1,0:T(2,128)(2,1)}), bf16[8,2,2048]{2,1,0:T(2,128)(2,1)S(1)}, u32[]{:S(2)}, u32[]{:S(2)}) async-start(bf16[8,2,2048]{2,1,0:T(2,128)(2,1)} %reshape.144), calls=%async_computation.3 | async-start | bytes 131072 | tf_op jit(solution)/shard_map/all_to_all | solution.py:92
  92.5 10.2 %all-to-all-start.2 = ((bf16[8,2,2048]{2,1,0:T(2,128)(2,1)}), bf16[8,2,2048]{2,1,0:T(2,128)(2,1)S(1)}, u32[]{:S(2)}, u32[]{:S(2)}) async-start(bf16[8,2,2048]{2,1,0:T(2,128)(2,1)} %reshape.142), calls=%async_computation.2 | async-start | bytes 131072 | tf_op jit(solution)/shard_map/all_to_all | solution.py:91
  103.3 1.1 copy-start.3
